TPU v7x, 512 devices: a whole 4x4x16 slice. The times are simulated.
512 devices in a mesh: grid: 64 (over y, z_lo, core), band: 8 (over z_hi, x).
Axes of the slice: x: 4, y: 4, z: 16 (z_hi: 2, z_lo: 8; z = z_hi * 8 + z_lo), core: 2. Of those that a mesh axis runs over, the one named last changes fastest.
Arguments:
- orbitals: bfloat16 [32, 64, 16, 32, 128], P('band', 'grid'), may hold values from -7 to 7
- occupations: float32 [32], P('band'), may hold values from 0.5 to 2
- density_in: float32 [64, 16, 32, 128], P('grid'), may hold values from 0.4 to 18
- history_in: bfloat16 [8, 64, 16, 32, 128], P(None, 'grid'), may hold values from 0.29882812 to 3
- history_res: bfloat16 [8, 64, 16, 32, 128], P(None, 'grid'), may hold values from -16 to 16
- screening: float32 [1], replicated, may hold values from 1.5 to 4
Outputs:
- density_next: float32 [64, 16, 32, 128], P('grid')
- residual: float32 [64, 16, 32, 128], P('grid')
All inputs are finite; a program needn't handle non-finite values.
Results may differ from a plain program's by a relative error of at most 0.0003.
Values sent between devices are 32-bit elements; how exact they have to be, the bound alone decides.
A program may use at most 64 MiB of HBM per device.

v0:
```python
import jax
import jax.numpy as jnp
from jax import lax
from jax.sharding import PartitionSpec as P

SWEEPS = 4
mixing_weight = 0.5


def partner(value, axis, apart):
    mask = 2**apart
    pairs = [(source, source ^ mask) for source in range(lax.axis_size(axis))]
    return lax.ppermute(value, axis, pairs)


def shifted(block, axis, distance):
    devices = range(lax.axis_size(axis))
    route = [(i - distance, i) for i in devices if i - distance in devices]
    return lax.ppermute(block, axis, route)


def fetch_whole(field, bit_list):
    for bit in bit_list:
        field = partner(field, "grid", bit)
    return field


def symmetrize(field, fetch, bits_x, bits_y, bits_z):
    field = 0.5 * (field + jnp.flip(fetch(field, bits_x), 1))
    field = 0.5 * (field + jnp.flip(fetch(field, bits_y), 2))
    field = 0.5 * (field + jnp.flip(fetch(field, bits_z), 3))
    return field


def neighbour(face, offset):
    return shifted(face, "grid", offset)


def local(orbitals, occupations, density_in, history_in, history_res, screening):
    n_grid = lax.axis_size("grid")
    grid_bits = n_grid.bit_length() - 1
    waves = orbitals.astype(jnp.float32)
    partial_value = jnp.sum(occupations[:, None, None, None, None] * waves * waves, 0)
    rho_out = lax.psum(partial_value, "band")
    rho_sym = symmetrize(rho_out, fetch_whole, list(range(4, grid_bits)), [2, 3], [0, 1])
    depth = history_res.shape[0]
    res_hist = history_res.astype(jnp.float32)
    charges = lax.psum(jnp.stack([jnp.sum(rho_sym), jnp.sum(density_in)]), "grid")
    scale = charges[1] / charges[0]
    residual = scale * rho_sym - density_in
    vectors = jnp.concatenate([res_hist, residual[None]], 0).reshape(depth + 1, -1)
    local_gram = jnp.dot(vectors, vectors.T, precision=lax.Precision.HIGHEST)
    gram = lax.psum(local_gram, "grid")
    lower = jnp.linalg.cholesky(gram)
    solved = jax.scipy.linalg.cho_solve((lower, True), jnp.ones((depth + 1,), jnp.float32))
    coefficients = solved / jnp.sum(solved)
    rho_opt = (
        jnp.einsum(
            "m,mgxyz->gxyz",
            coefficients[:depth],
            history_in.astype(jnp.float32),
            precision=lax.Precision.HIGHEST,
        )
        + coefficients[depth] * density_in
    )
    res_opt = (
        jnp.einsum("m,mgxyz->gxyz", coefficients[:depth], res_hist, precision=lax.Precision.HIGHEST)
        + coefficients[depth] * residual
    )
    kappa = screening[0]
    index = lax.axis_index("grid")
    block_x = index // 16
    block_y = index // 4 % 4
    block_z = index % 4
    keep_xlow = (block_x > 0).astype(jnp.float32)
    keep_ylow = (block_y > 0).astype(jnp.float32)
    keep_yhigh = (block_y < 3).astype(jnp.float32)
    keep_zlow = (block_z > 0).astype(jnp.float32)
    keep_zhigh = (block_z < 3).astype(jnp.float32)
    source = res_opt[0]
    field_u = jnp.zeros_like(source)
    for sweep in range(SWEEPS):
        x_low = neighbour(field_u[-1:], 16) * keep_xlow
        x_high = neighbour(field_u[:1], -16)
        y_low = neighbour(field_u[:, -1:], 4) * keep_ylow
        y_high = neighbour(field_u[:, :1], -4) * keep_yhigh
        z_low = neighbour(field_u[:, :, -1:], 1) * keep_zlow
        z_high = neighbour(field_u[:, :, :1], -1) * keep_zhigh
        along_x = jnp.concatenate([x_low, field_u, x_high], 0)
        along_y = jnp.concatenate([y_low, field_u, y_high], 1)
        along_z = jnp.concatenate([z_low, field_u, z_high], 2)
        beside = along_x[:-2] + along_x[2:]
        beside = beside + along_y[:, :-2] + along_y[:, 2:]
        beside = beside + along_z[:, :, :-2] + along_z[:, :, 2:]
        field_u = (source + beside) / (6.0 + kappa)
    density_next = rho_opt + mixing_weight * (res_opt - kappa * field_u[None])
    return (density_next, residual)


def solution(mesh):
    in_specs = (
        P("band", "grid", None, None, None),
        P("band"),
        P("grid", None, None, None),
        P(None, "grid", None, None, None),
        P(None, "grid", None, None, None),
        P(),
    )
    out_specs = (P("grid", None, None, None), P("grid", None, None, None))
    return jax.shard_map(local, mesh=mesh, in_specs=in_specs, out_specs=out_specs, check_vma=False)
```

profile of v0, /device:TPU:8, one launch (start us, length us, event | category | flops | bytes accessed | tf_op | source)
XLA Modules:
  0.0 786.0 jit_solution(13246422287680302552)
XLA Ops:
  7.2 2.1 fusion.4
  9.4 158.1 %all-reduce.8.cloned.1.call-done = f32[1,16,32,128]{3,2,1,0:T(8,128)} async-done(((f32[1,16,32,128]{3,2,1,0:T(8,128)}), f32[1,16,32,128]{3,2,1,0:T(8,128)}) %all-reduce.8.cloned.1.call-update) | async-done | bytes 262160 | tf_op jit(solution)/shard_map/psum | solution.py:44
  167.6 2.4 collective-permute-start
  170.0 6.6 collective-permute-done
  176.6 6.1 collective-permute-start.1
  182.8 4.3 collective-permute-done.1
  188.1 2.5 collective-permute-start.2
  190.7 4.4 collective-permute-start.9
  195.1 2.3 collective-permute-start.8
  198.2 2.5 collective-permute-start.11
  200.7 1.9 collective-permute-start.10
  204.0 4.8 collective-permute-start.3
  208.8 1.9 copy_convert_fusion
  210.7 27.2 %collective-permute-done.3 = f32[1,16,32,128]{3,2,1,0:T(8,128)S(1)} collective-permute-done((f32[1,16,32,128]{3,2,1,0:T(8,128)S(1)}, f32[1,16,32,128]{3,2,1,0:T(8,128)S(1)}, u32[]{:S(2)}, u32[]{:S(2)}) %collective-permute-start.3) | collective-permute-done | bytes 262176 | tf_op jit(solution)/shard_map/ppermute | solution.py:13
  237.9 3.8 collective-permute-start.6
  241.9 1.9 collective-permute-start.4
  244.8 2.0 collective-permute-start.7
  246.8 1.9 collective-permute-start.5
  248.8 8.7 %collective-permute-done.5 = f32[1,16,32,128]{3,2,1,0:T(8,128)} collective-permute-done((f32[1,16,32,128]{3,2,1,0:T(8,128)S(1)}, f32[1,16,32,128]{3,2,1,0:T(8,128)}, u32[]{:S(2)}, u32[]{:S(2)}) %collective-permute-start.5) | collective-permute-done | bytes 262176 | tf_op jit(solution)/shard_map/ppermute | solution.py:13
  258.6 1.3 multiply_reduce_fusion
  259.9 1.3 pad_maximum_fusion.18
  261.2 191.7 %psum.22 = f32[2]{0:T(128)S(1)} all-reduce(f32[2]{0:T(128)S(1)} %pad_maximum_fusion.18), channel_id=1, replica_groups=mesh['grid'=64,'band'=8] {'grid'}, use_global_device_ids=true, to_apply=%region_4.5 | all-reduce | flops 2 | bytes 16 | tf_op jit(solution)/shard_map/psum | solution.py:48
  455.9 7.9 %fusion.3 = f32[9,9]{0,1:T(8,128)S(1)} fusion(f32[1,1,16,32,128]{4,0,3,2,1:T(1,128)S(1)} %bitcast.88, f32[8,1,16,32,128]{4,0,3,2,1:T(8,128)} %copy_convert_fusion), kind=kOutput, calls=%fused_computation.5 | convolution fusion | flops 64290816 | bytes 2359620 | tf_op jit(solution)/shard_map/dot_general | solution.py:52
  463.8 193.5 %psum.23 = f32[9,9]{0,1:T(8,128)S(1)} all-reduce(f32[9,9]{0,1:T(8,128)S(1)} %fusion.3), channel_id=1, replica_groups=mesh['grid'=64,'band'=8] {'grid'}, use_global_device_ids=true, to_apply=%region_5.6 | all-reduce | flops 81 | bytes 648 | tf_op jit(solution)/shard_map/psum | solution.py:53
  661.9 1.3 fusion.5
  664.8 1.9 collective-permute-start.16
  666.7 11.1 %collective-permute-start.17 = (f32[16,32,1]{2,1,0:T(8,128)S(1)}, f32[16,32,1]{2,1,0:T(8,128)S(1)}, u32[]{:S(2)}, u32[]{:S(2)}) collective-permute-start(f32[16,32,1]{2,1,0:T(8,128)S(1)} %get-tuple-element.23), channel_id=1, source_target_pairs={{8,0},{16,8},{24,16},{32,24},{40,32},{48,40},{56,48},{64,56},{72,6... | collective-permute-start | bytes 6152 | tf_op jit(solution)/shard_map/ppermute | solution.py:19
  677.9 1.9 collective-permute-start.15
  679.8 4.8 collective-permute-start.14
  684.6 4.4 collective-permute-start.12
  689.1 1.3 fusion.7
  690.4 30.0 %collective-permute-start.13 = (f32[1,32,128]{2,1,0:T(8,128)S(1)}, f32[1,32,128]{2,1,0:T(8,128)S(1)}, u32[]{:S(2)}, u32[]{:S(2)}) collective-permute-start(f32[1,32,128]{2,1,0:T(8,128)S(1)} %get-tuple-element.19), channel_id=1, source_target_pairs={{128,0},{136,8},{144,16},{152,24},{160,32},{168,40},{176,48},{184,... | collective-permute-start | bytes 49160 | tf_op jit(solution)/shard_map/ppermute | solution.py:19
  720.5 1.3 collective-permute-done.13
  722.2 1.9 collective-permute-start.22
  724.2 11.1 %collective-permute-start.23 = (f32[16,32,1]{2,1,0:T(8,128)S(1)}, f32[16,32,1]{2,1,0:T(8,128)S(1)}, u32[]{:S(2)}, u32[]{:S(2)}) collective-permute-start(f32[16,32,1]{2,1,0:T(8,128)S(1)} %get-tuple-element.17), channel_id=1, source_target_pairs={{8,0},{16,8},{24,16},{32,24},{40,32},{48,40},{56,48},{64,56},{72,6... | collective-permute-start | bytes 6152 | tf_op jit(solution)/shard_map/ppermute | solution.py:19
  735.3 1.9 collective-permute-start.21
  737.3 4.8 collective-permute-start.20
  742.1 1.9 collective-permute-start.18
  744.0 3.9 collective-permute-start.19
  748.1 1.4 collective-permute-done.20
  750.1 1.9 collective-permute-start.28
  752.0 11.1 %collective-permute-start.29 = (f32[16,32,1]{2,1,0:T(8,128)S(1)}, f32[16,32,1]{2,1,0:T(8,128)S(1)}, u32[]{:S(2)}, u32[]{:S(2)}) collective-permute-start(f32[16,32,1]{2,1,0:T(8,128)S(1)} %get-tuple-element.11), channel_id=1, source_target_pairs={{8,0},{16,8},{24,16},{32,24},{40,32},{48,40},{56,48},{64,56},{72,6... | collective-permute-start | bytes 6152 | tf_op jit(solution)/shard_map/ppermute | solution.py:19
  763.2 1.9 collective-permute-start.27
  765.1 4.8 collective-permute-start.26
  770.0 1.9 collective-permute-start.24
  771.9 3.9 collective-permute-start.25
  775.9 1.4 collective-permute-done.26
  777.5 1.6 fusion.23
  (86 shorter events, 13.9 us)
Async XLA Ops:
  7.2 681.9 %copy-start = (bf16[8,1,16,32,128]{4,3,2,1,0:T(8,128)(2,1)S(1)}, bf16[8,1,16,32,128]{4,3,2,1,0:T(8,128)(2,1)}, u32[]{:S(2)}) copy-start(bf16[8,1,16,32,128]{4,3,2,1,0:T(8,128)(2,1)} %param.9) | copy-start | bytes 3145732
  7.2 195.5 %copy-start.2 = (f32[1,16,32,128]{3,2,1,0:T(8,128)S(1)}, f32[1,16,32,128]{3,2,1,0:T(8,128)}, u32[]{:S(2)}) copy-start(f32[1,16,32,128]{3,2,1,0:T(8,128)} %param.8) | copy-start | bytes 786436
  7.2 201.6 %copy-start.1 = (bf16[8,1,16,32,128]{4,3,2,1,0:T(8,128)(2,1)S(1)}, bf16[8,1,16,32,128]{4,3,2,1,0:T(8,128)(2,1)}, u32[]{:S(2)}) copy-start(bf16[8,1,16,32,128]{4,3,2,1,0:T(8,128)(2,1)} %param.10) | copy-start | bytes 3145732
  7.2 160.4 %all-reduce.8.cloned.1.call-start = ((), (), s32[]{:S(2)}) async-start(), calls=%async_computation | async-start | bytes 524288 | tf_op jit(solution)/shard_map/psum | solution.py:44
  167.6 9.1 %collective-permute-start = (f32[1,16,32,128]{3,2,1,0:T(8,128)}, f32[1,16,32,128]{3,2,1,0:T(8,128)S(1)}, u32[]{:S(2)}, u32[]{:S(2)}) collective-permute-start(f32[1,16,32,128]{3,2,1,0:T(8,128)} %all-reduce.8.cloned.1.call-done), channel_id=1, source_target_pairs={{0,128},{8,136},{16,144},{24,152},{32,160},{40,168},{48,176},{56,1... | collective-permute-start | bytes 786440 | tf_op jit(solution)/shard_map/ppermute | solution.py:13
  176.6 10.5 %collective-permute-start.1 = (f32[1,16,32,128]{3,2,1,0:T(8,128)S(1)}, f32[1,16,32,128]{3,2,1,0:T(8,128)S(1)}, u32[]{:S(2)}, u32[]{:S(2)}) collective-permute-start(f32[1,16,32,128]{3,2,1,0:T(8,128)S(1)} %collective-permute-done), channel_id=1, source_target_pairs={{0,256},{8,264},{16,272},{24,280},{32,288},{40,296},{48,304},{56,3... | collective-permute-start | bytes 786440 | tf_op jit(solution)/shard_map/ppermute | solution.py:13
  188.1 15.9 %collective-permute-start.2 = (f32[1,16,32,128]{3,2,1,0:T(8,128)S(1)}, f32[1,16,32,128]{3,2,1,0:T(8,128)S(1)}, u32[]{:S(2)}, u32[]{:S(2)}) collective-permute-start(f32[1,16,32,128]{3,2,1,0:T(8,128)S(1)} %add_multiply_fusion.1), channel_id=1, source_target_pairs={{0,32},{8,40},{16,48},{24,56},{32,0},{40,8},{48,16},{56,24},{64,96... | collective-permute-start | bytes 786440 | tf_op jit(solution)/shard_map/ppermute | solution.py:13
  190.7 58.1 %collective-permute-start.9 = (f32[16,1,128]{2,1,0:T(1,128)S(1)}, f32[16,1,128]{2,1,0:T(1,128)S(1)}, u32[]{:S(2)}, u32[]{:S(2)}) collective-permute-start(f32[16,1,128]{2,1,0:T(1,128)S(1)} %broadcast.113), channel_id=1, source_target_pairs={{32,0},{40,8},{48,16},{56,24},{64,32},{72,40},{80,48},{88,56},{96,... | collective-permute-start | bytes 24584 | tf_op jit(solution)/shard_map/ppermute | solution.py:19
  195.1 53.7 %collective-permute-start.8 = (f32[16,1,128]{2,1,0:T(1,128)S(1)}, f32[16,1,128]{2,1,0:T(1,128)S(1)}, u32[]{:S(2)}, u32[]{:S(2)}) collective-permute-start(f32[16,1,128]{2,1,0:T(1,128)S(1)} %broadcast.113), channel_id=1, source_target_pairs={{0,32},{8,40},{16,48},{24,56},{32,64},{40,72},{48,80},{56,88},{64,... | collective-permute-start | bytes 24584 | tf_op jit(solution)/shard_map/ppermute | solution.py:19
  198.2 43.7 %collective-permute-start.11 = (f32[16,32,1]{2,1,0:T(8,128)}, f32[16,32,1]{2,1,0:T(8,128)}, u32[]{:S(2)}, u32[]{:S(2)}) collective-permute-start(f32[16,32,1]{2,1,0:T(8,128)} %broadcast.114), channel_id=1, source_target_pairs={{8,0},{16,8},{24,16},{32,24},{40,32},{48,40},{56,48},{64,56},{72,6... | collective-permute-start | bytes 6152 | tf_op jit(solution)/shard_map/ppermute | solution.py:19
  200.7 44.1 %collective-permute-start.10 = (f32[16,32,1]{2,1,0:T(8,128)}, f32[16,32,1]{2,1,0:T(8,128)S(1)}, u32[]{:S(2)}, u32[]{:S(2)}) collective-permute-start(f32[16,32,1]{2,1,0:T(8,128)} %broadcast.114), channel_id=1, source_target_pairs={{0,8},{8,16},{16,24},{24,32},{32,40},{40,48},{48,56},{56,64},{64,7... | collective-permute-start | bytes 6152 | tf_op jit(solution)/shard_map/ppermute | solution.py:19
  204.0 33.9 %collective-permute-start.3 = (f32[1,16,32,128]{3,2,1,0:T(8,128)S(1)}, f32[1,16,32,128]{3,2,1,0:T(8,128)S(1)}, u32[]{:S(2)}, u32[]{:S(2)}) collective-permute-start(f32[1,16,32,128]{3,2,1,0:T(8,128)S(1)} %collective-permute-done.2), channel_id=1, source_target_pairs={{0,64},{8,72},{16,80},{24,88},{32,96},{40,104},{48,112},{56,120},{... | collective-permute-start | bytes 786440 | tf_op jit(solution)/shard_map/ppermute | solution.py:13
  237.9 23.3 %collective-permute-start.6 = (f32[1,32,128]{2,1,0:T(8,128)S(1)}, f32[1,32,128]{2,1,0:T(8,128)S(1)}, u32[]{:S(2)}, u32[]{:S(2)}) collective-permute-start(f32[1,32,128]{2,1,0:T(8,128)S(1)} %broadcast.112), channel_id=1, source_target_pairs={{0,128},{8,136},{16,144},{24,152},{32,160},{40,168},{48,176},{56,1... | collective-permute-start | bytes 49160 | tf_op jit(solution)/shard_map/ppermute | solution.py:19
  241.9 4.9 collective-permute-start.4
  244.8 419.0 %collective-permute-start.7 = (f32[1,32,128]{2,1,0:T(8,128)S(1)}, f32[1,32,128]{2,1,0:T(8,128)S(1)}, u32[]{:S(2)}, u32[]{:S(2)}) collective-permute-start(f32[1,32,128]{2,1,0:T(8,128)S(1)} %broadcast.112), channel_id=1, source_target_pairs={{128,0},{136,8},{144,16},{152,24},{160,32},{168,40},{176,48},{184,... | collective-permute-start | bytes 49160 | tf_op jit(solution)/shard_map/ppermute | solution.py:19
  246.8 10.7 %collective-permute-start.5 = (f32[1,16,32,128]{3,2,1,0:T(8,128)S(1)}, f32[1,16,32,128]{3,2,1,0:T(8,128)}, u32[]{:S(2)}, u32[]{:S(2)}) collective-permute-start(f32[1,16,32,128]{3,2,1,0:T(8,128)S(1)} %collective-permute-done.4), channel_id=1, source_target_pairs={{0,16},{8,24},{16,0},{24,8},{32,48},{40,56},{48,32},{56,40},{64,80... | collective-permute-start | bytes 786440 | tf_op jit(solution)/shard_map/ppermute | solution.py:13
  455.9 207.9 %copy-start.3 = (f32[1,16,32,128]{3,2,1,0:T(8,128)}, f32[1,16,32,128]{3,2,1,0:T(8,128)S(1)}, u32[]{:S(2)}) copy-start(f32[1,16,32,128]{3,2,1,0:T(8,128)S(1)} %multiply_subtract_fusion) | copy-start | bytes 786436
  664.8 25.6 %collective-permute-start.16 = (f32[16,32,1]{2,1,0:T(8,128)S(1)}, f32[16,32,1]{2,1,0:T(8,128)S(1)}, u32[]{:S(2)}, u32[]{:S(2)}) collective-permute-start(f32[16,32,1]{2,1,0:T(8,128)S(1)} %get-tuple-element.22), channel_id=1, source_target_pairs={{0,8},{8,16},{16,24},{24,32},{32,40},{40,48},{48,56},{56,64},{64,7... | collective-permute-start | bytes 6152 | tf_op jit(solution)/shard_map/ppermute | solution.py:19
  666.7 53.7 %collective-permute-start.17 = (f32[16,32,1]{2,1,0:T(8,128)S(1)}, f32[16,32,1]{2,1,0:T(8,128)S(1)}, u32[]{:S(2)}, u32[]{:S(2)}) collective-permute-start(f32[16,32,1]{2,1,0:T(8,128)S(1)} %get-tuple-element.23), channel_id=1, source_target_pairs={{8,0},{16,8},{24,16},{32,24},{40,32},{48,40},{56,48},{64,56},{72,6... | collective-permute-start | bytes 6152 | tf_op jit(solution)/shard_map/ppermute | solution.py:19
  677.9 42.6 %collective-permute-start.15 = (f32[16,1,128]{2,1,0:T(1,128)S(1)}, f32[16,1,128]{2,1,0:T(1,128)S(1)}, u32[]{:S(2)}, u32[]{:S(2)}) collective-permute-start(f32[16,1,128]{2,1,0:T(1,128)S(1)} %get-tuple-element.21), channel_id=1, source_target_pairs={{32,0},{40,8},{48,16},{56,24},{64,32},{72,40},{80,48},{88,56},{96,... | collective-permute-start | bytes 24584 | tf_op jit(solution)/shard_map/ppermute | solution.py:19
  679.8 40.7 %collective-permute-start.14 = (f32[16,1,128]{2,1,0:T(1,128)S(1)}, f32[16,1,128]{2,1,0:T(1,128)S(1)}, u32[]{:S(2)}, u32[]{:S(2)}) collective-permute-start(f32[16,1,128]{2,1,0:T(1,128)S(1)} %get-tuple-element.20), channel_id=1, source_target_pairs={{0,32},{8,40},{16,48},{24,56},{32,64},{40,72},{48,80},{56,88},{64,... | collective-permute-start | bytes 24584 | tf_op jit(solution)/shard_map/ppermute | solution.py:19
  684.6 35.9 %collective-permute-start.12 = (f32[1,32,128]{2,1,0:T(8,128)S(1)}, f32[1,32,128]{2,1,0:T(8,128)S(1)}, u32[]{:S(2)}, u32[]{:S(2)}) collective-permute-start(f32[1,32,128]{2,1,0:T(8,128)S(1)} %get-tuple-element.18), channel_id=1, source_target_pairs={{0,128},{8,136},{16,144},{24,152},{32,160},{40,168},{48,176},{56,1... | collective-permute-start | bytes 49160 | tf_op jit(solution)/shard_map/ppermute | solution.py:19
  690.4 31.4 %collective-permute-start.13 = (f32[1,32,128]{2,1,0:T(8,128)S(1)}, f32[1,32,128]{2,1,0:T(8,128)S(1)}, u32[]{:S(2)}, u32[]{:S(2)}) collective-permute-start(f32[1,32,128]{2,1,0:T(8,128)S(1)} %get-tuple-element.19), channel_id=1, source_target_pairs={{128,0},{136,8},{144,16},{152,24},{160,32},{168,40},{176,48},{184,... | collective-permute-start | bytes 49160 | tf_op jit(solution)/shard_map/ppermute | solution.py:19
  722.2 21.8 %collective-permute-start.22 = (f32[16,32,1]{2,1,0:T(8,128)S(1)}, f32[16,32,1]{2,1,0:T(8,128)S(1)}, u32[]{:S(2)}, u32[]{:S(2)}) collective-permute-start(f32[16,32,1]{2,1,0:T(8,128)S(1)} %get-tuple-element.16), channel_id=1, source_target_pairs={{0,8},{8,16},{16,24},{24,32},{32,40},{40,48},{48,56},{56,64},{64,7... | collective-permute-start | bytes 6152 | tf_op jit(solution)/shard_map/ppermute | solution.py:19
  724.2 23.8 %collective-permute-start.23 = (f32[16,32,1]{2,1,0:T(8,128)S(1)}, f32[16,32,1]{2,1,0:T(8,128)S(1)}, u32[]{:S(2)}, u32[]{:S(2)}) collective-permute-start(f32[16,32,1]{2,1,0:T(8,128)S(1)} %get-tuple-element.17), channel_id=1, source_target_pairs={{8,0},{16,8},{24,16},{32,24},{40,32},{48,40},{56,48},{64,56},{72,6... | collective-permute-start | bytes 6152 | tf_op jit(solution)/shard_map/ppermute | solution.py:19
  735.3 12.7 %collective-permute-start.21 = (f32[16,1,128]{2,1,0:T(1,128)S(1)}, f32[16,1,128]{2,1,0:T(1,128)S(1)}, u32[]{:S(2)}, u32[]{:S(2)}) collective-permute-start(f32[16,1,128]{2,1,0:T(1,128)S(1)} %get-tuple-element.15), channel_id=1, source_target_pairs={{32,0},{40,8},{48,16},{56,24},{64,32},{72,40},{80,48},{88,56},{96,... | collective-permute-start | bytes 24584 | tf_op jit(solution)/shard_map/ppermute | solution.py:19
  737.3 12.1 %collective-permute-start.20 = (f32[16,1,128]{2,1,0:T(1,128)S(1)}, f32[16,1,128]{2,1,0:T(1,128)S(1)}, u32[]{:S(2)}, u32[]{:S(2)}) collective-permute-start(f32[16,1,128]{2,1,0:T(1,128)S(1)} %get-tuple-element.14), channel_id=1, source_target_pairs={{0,32},{8,40},{16,48},{24,56},{32,64},{40,72},{48,80},{56,88},{64,... | collective-permute-start | bytes 24584 | tf_op jit(solution)/shard_map/ppermute | solution.py:19
  742.1 7.3 collective-permute-start.18
  744.0 5.6 collective-permute-start.19
  750.1 21.8 %collective-permute-start.28 = (f32[16,32,1]{2,1,0:T(8,128)S(1)}, f32[16,32,1]{2,1,0:T(8,128)S(1)}, u32[]{:S(2)}, u32[]{:S(2)}) collective-permute-start(f32[16,32,1]{2,1,0:T(8,128)S(1)} %get-tuple-element.10), channel_id=1, source_target_pairs={{0,8},{8,16},{16,24},{24,32},{32,40},{40,48},{48,56},{56,64},{64,7... | collective-permute-start | bytes 6152 | tf_op jit(solution)/shard_map/ppermute | solution.py:19
  752.0 23.8 %collective-permute-start.29 = (f32[16,32,1]{2,1,0:T(8,128)S(1)}, f32[16,32,1]{2,1,0:T(8,128)S(1)}, u32[]{:S(2)}, u32[]{:S(2)}) collective-permute-start(f32[16,32,1]{2,1,0:T(8,128)S(1)} %get-tuple-element.11), channel_id=1, source_target_pairs={{8,0},{16,8},{24,16},{32,24},{40,32},{48,40},{56,48},{64,56},{72,6... | collective-permute-start | bytes 6152 | tf_op jit(solution)/shard_map/ppermute | solution.py:19
  763.2 12.7 %collective-permute-start.27 = (f32[16,1,128]{2,1,0:T(1,128)S(1)}, f32[16,1,128]{2,1,0:T(1,128)S(1)}, u32[]{:S(2)}, u32[]{:S(2)}) collective-permute-start(f32[16,1,128]{2,1,0:T(1,128)S(1)} %get-tuple-element.9), channel_id=1, source_target_pairs={{32,0},{40,8},{48,16},{56,24},{64,32},{72,40},{80,48},{88,56},{96,... | collective-permute-start | bytes 24584 | tf_op jit(solution)/shard_map/ppermute | solution.py:19
  765.1 12.1 %collective-permute-start.26 = (f32[16,1,128]{2,1,0:T(1,128)S(1)}, f32[16,1,128]{2,1,0:T(1,128)S(1)}, u32[]{:S(2)}, u32[]{:S(2)}) collective-permute-start(f32[16,1,128]{2,1,0:T(1,128)S(1)} %get-tuple-element.8), channel_id=1, source_target_pairs={{0,32},{8,40},{16,48},{24,56},{32,64},{40,72},{48,80},{56,88},{64,... | collective-permute-start | bytes 24584 | tf_op jit(solution)/shard_map/ppermute | solution.py:19
  770.0 7.3 collective-permute-start.24
  771.9 5.6 collective-permute-start.25
Sparse Core Ops, SparseCore 0:
  11.5 155.9 all-reduce.7
where the time goes:
time: 787 us; the launch traced here: 786 us
  blocking collectives  385 us (49%)
  waiting for transfers between devices  210 us (27%)
  starting transfers between devices  142 us (18%)
  other arithmetic  17 us (2%)
  between operations  16.8 us (2%)
  matrix products  11.4 us (1%)
    psum x1, blocking collectives, local(): gram = lax.psum(local_gram, 'grid')  194 us
    psum x1, blocking collectives, local(): lax.psum(jnp.stack([jnp.sum(rho_sym), jnp.sum(density_in)]), 'grid')  192 us
    psum x1, waiting for transfers between devices, local(): rho_out = lax.psum(partial_value, 'band')  158 us
    ppermute x24, starting transfers between devices, shifted(): return lax.ppermute(block, axis, route)  123 us
    ppermute x6, waiting for transfers between devices, partner(): return lax.ppermute(value, axis, pairs)  46.9 us
    ppermute x6, starting transfers between devices, partner(): return lax.ppermute(value, axis, pairs)  19.7 us
  transfers between devices with their start and end apart: 31, of which 10 were waited for; matrix products, arithmetic and copies ran while one was open for 3% of the time, Pallas kernels for 0%

commit v1 on v0

--- a/solution.py
+++ b/solution.py
@@ -41,7 +41,7 @@
     grid_bits = n_grid.bit_length() - 1
     waves = orbitals.astype(jnp.float32)
     partial_value = jnp.sum(occupations[:, None, None, None, None] * waves * waves, 0)
-    rho_out = lax.psum(partial_value, "band")
+    rho_out = jnp.sum(lax.all_gather(partial_value, "band"), axis=0)
     rho_sym = symmetrize(rho_out, fetch_whole, list(range(4, grid_bits)), [2, 3], [0, 1])
     depth = history_res.shape[0]
     res_hist = history_res.astype(jnp.float32)

time: 787 us -> 756 us (0.961)
  the two profiles are of different devices: /device:TPU:8 before, /device:TPU:2 now
where the time goes in v1:
time: 756 us; the launch traced here: 754 us
  blocking collectives  426 us (56%)
  waiting for transfers between devices  185 us (24%)
  starting transfers between devices  93.3 us (12%)
  other arithmetic  17.8 us (2%)
  between operations  16.8 us (2%)
  matrix products  11.4 us (2%)
    psum x1, blocking collectives, local(): lax.psum(jnp.stack([jnp.sum(rho_sym), jnp.sum(density_in)]), 'grid')  213 us
    psum x1, blocking collectives, local(): gram = lax.psum(local_gram, 'grid')  213 us
    all_gather x1, waiting for transfers between devices, local(): rho_out = jnp.sum(lax.all_gather(partial_value, 'band'), axis=0)  124 us
    ppermute x24, starting transfers between devices, shifted(): return lax.ppermute(block, axis, route)  76.3 us
    ppermute x6, waiting for transfers between devices, partner(): return lax.ppermute(value, axis, pairs)  49 us
    ppermute x6, starting transfers between devices, partner(): return lax.ppermute(value, axis, pairs)  16.9 us
  transfers between devices with their start and end apart: 31, of which 8 were waited for; matrix products, arithmetic and copies ran while one was open for 3% of the time, Pallas kernels for 0%

profile of v1, /device:TPU:2, one launch (start us, length us, event | category | flops | bytes accessed | tf_op | source)
XLA Modules:
  0.0 754.4 jit_solution(35098139547245458)
XLA Ops:
  7.2 2.1 fusion.4
  9.4 123.7 %all-gather.3.cloned.1.call-done = f32[128,32,128]{2,1,0:T(8,128)} async-done(((f32[16,32,128]{2,1,0:T(8,128)}), f32[128,32,128]{2,1,0:T(8,128)}) %all-gather.3.cloned.1.call-update) | async-done | bytes 2097168 | tf_op jit(solution)/shard_map/all_gather | solution.py:44
  133.1 1.8 reduce.8
  134.9 2.7 collective-permute-start
  137.6 6.9 collective-permute-done
  144.5 3.0 collective-permute-start.1
  147.5 7.2 collective-permute-done.1
  154.7 2.3 collective-permute-start.2
  157.0 1.3 collective-permute-start.9
  158.3 5.4 collective-permute-start.8
  164.5 1.3 collective-permute-start.11
  165.8 3.0 collective-permute-start.10
  170.2 5.1 collective-permute-start.3
  175.3 1.9 copy_convert_fusion
  177.2 26.2 %collective-permute-done.3 = f32[1,16,32,128]{3,2,1,0:T(8,128)S(1)} collective-permute-done((f32[1,16,32,128]{3,2,1,0:T(8,128)S(1)}, f32[1,16,32,128]{3,2,1,0:T(8,128)S(1)}, u32[]{:S(2)}, u32[]{:S(2)}) %collective-permute-start.3) | collective-permute-done | bytes 262176 | tf_op jit(solution)/shard_map/ppermute | solution.py:13
  203.5 5.9 collective-permute-start.6
  209.6 1.9 collective-permute-start.4
  212.5 1.3 collective-permute-start.7
  213.8 1.9 collective-permute-start.5
  215.8 8.7 %collective-permute-done.5 = f32[1,16,32,128]{3,2,1,0:T(8,128)} collective-permute-done((f32[1,16,32,128]{3,2,1,0:T(8,128)S(1)}, f32[1,16,32,128]{3,2,1,0:T(8,128)}, u32[]{:S(2)}, u32[]{:S(2)}) %collective-permute-start.5) | collective-permute-done | bytes 262176 | tf_op jit(solution)/shard_map/ppermute | solution.py:13
  225.6 1.3 multiply_reduce_fusion
  226.9 1.3 pad_maximum_fusion.18
  228.2 213.2 %psum.14 = f32[2]{0:T(128)S(1)} all-reduce(f32[2]{0:T(128)S(1)} %pad_maximum_fusion.18), channel_id=1, replica_groups=mesh['grid'=64,'band'=8] {'grid'}, use_global_device_ids=true, to_apply=%region_4.5 | all-reduce | flops 2 | bytes 16 | tf_op jit(solution)/shard_map/psum | solution.py:48
  444.4 8.0 %fusion.3 = f32[9,9]{0,1:T(8,128)S(1)} fusion(f32[1,1,16,32,128]{4,0,3,2,1:T(1,128)S(1)} %bitcast.91, f32[8,1,16,32,128]{4,0,3,2,1:T(8,128)} %copy_convert_fusion), kind=kOutput, calls=%fused_computation.5 | convolution fusion | flops 64290816 | bytes 2359620 | tf_op jit(solution)/shard_map/dot_general | solution.py:52
  452.3 212.8 %psum.15 = f32[9,9]{0,1:T(8,128)S(1)} all-reduce(f32[9,9]{0,1:T(8,128)S(1)} %fusion.3), channel_id=1, replica_groups=mesh['grid'=64,'band'=8] {'grid'}, use_global_device_ids=true, to_apply=%region_5.6 | all-reduce | flops 81 | bytes 648 | tf_op jit(solution)/shard_map/psum | solution.py:53
  669.6 1.3 fusion.5
  672.5 1.6 collective-permute-start.16
  674.2 1.3 collective-permute-start.17
  675.5 1.3 collective-permute-start.15
  676.8 5.4 collective-permute-start.14
  682.2 1.3 collective-permute-start.12
  684.8 1.3 collective-permute-start.13
  686.2 4.2 collective-permute-done.13
  690.9 1.3 collective-permute-start.22
  692.2 1.3 collective-permute-start.23
  693.5 1.3 collective-permute-start.21
  694.8 5.5 collective-permute-start.20
  700.4 12.0 %collective-permute-start.18 = (f32[1,32,128]{2,1,0:T(8,128)S(1)}, f32[1,32,128]{2,1,0:T(8,128)S(1)}, u32[]{:S(2)}, u32[]{:S(2)}) collective-permute-start(f32[1,32,128]{2,1,0:T(8,128)S(1)} %get-tuple-element.12), channel_id=1, source_target_pairs={{0,128},{8,136},{16,144},{24,152},{32,160},{40,168},{48,176},{56,1... | collective-permute-start | bytes 49160 | tf_op jit(solution)/shard_map/ppermute | solution.py:19
  712.4 1.3 collective-permute-start.19
  713.8 4.2 collective-permute-done.19
  718.5 1.3 collective-permute-start.28
  719.8 1.3 collective-permute-start.29
  721.1 1.3 collective-permute-start.27
  722.4 5.5 collective-permute-start.26
  727.9 12.3 %collective-permute-start.24 = (f32[1,32,128]{2,1,0:T(8,128)S(1)}, f32[1,32,128]{2,1,0:T(8,128)S(1)}, u32[]{:S(2)}, u32[]{:S(2)}) collective-permute-start(f32[1,32,128]{2,1,0:T(8,128)S(1)} %get-tuple-element.6), channel_id=1, source_target_pairs={{0,128},{8,136},{16,144},{24,152},{32,160},{40,168},{48,176},{56,1... | collective-permute-start | bytes 49160 | tf_op jit(solution)/shard_map/ppermute | solution.py:19
  740.3 1.3 collective-permute-start.25
  741.7 4.2 collective-permute-done.25
  745.9 1.6 fusion.23
  (87 shorter events, 13.7 us)
Async XLA Ops:
  7.2 676.4 %copy-start = (bf16[8,1,16,32,128]{4,3,2,1,0:T(8,128)(2,1)S(1)}, bf16[8,1,16,32,128]{4,3,2,1,0:T(8,128)(2,1)}, u32[]{:S(2)}) copy-start(bf16[8,1,16,32,128]{4,3,2,1,0:T(8,128)(2,1)} %param.9) | copy-start | bytes 3145732
  7.2 161.7 %copy-start.2 = (f32[1,16,32,128]{3,2,1,0:T(8,128)S(1)}, f32[1,16,32,128]{3,2,1,0:T(8,128)}, u32[]{:S(2)}) copy-start(f32[1,16,32,128]{3,2,1,0:T(8,128)} %param.8) | copy-start | bytes 786436
  7.2 125.9 %all-gather.3.cloned.1.call-start = ((), (), s32[]{:S(2)}) async-start(), calls=%async_computation | async-start | bytes 2359296 | tf_op jit(solution)/shard_map/all_gather | solution.py:44
  9.3 166.0 %copy-start.1 = (bf16[8,1,16,32,128]{4,3,2,1,0:T(8,128)(2,1)S(1)}, bf16[8,1,16,32,128]{4,3,2,1,0:T(8,128)(2,1)}, u32[]{:S(2)}) copy-start(bf16[8,1,16,32,128]{4,3,2,1,0:T(8,128)(2,1)} %param.10) | copy-start | bytes 3145732
  134.9 9.6 %collective-permute-start = (f32[1,16,32,128]{3,2,1,0:T(8,128)S(1)}, f32[1,16,32,128]{3,2,1,0:T(8,128)S(1)}, u32[]{:S(2)}, u32[]{:S(2)}) collective-permute-start(f32[1,16,32,128]{3,2,1,0:T(8,128)S(1)} %bitcast.88), channel_id=1, source_target_pairs={{0,128},{8,136},{16,144},{24,152},{32,160},{40,168},{48,176},{56,1... | collective-permute-start | bytes 786440 | tf_op jit(solution)/shard_map/ppermute | solution.py:13
  144.5 10.1 %collective-permute-start.1 = (f32[1,16,32,128]{3,2,1,0:T(8,128)S(1)}, f32[1,16,32,128]{3,2,1,0:T(8,128)S(1)}, u32[]{:S(2)}, u32[]{:S(2)}) collective-permute-start(f32[1,16,32,128]{3,2,1,0:T(8,128)S(1)} %collective-permute-done), channel_id=1, source_target_pairs={{0,256},{8,264},{16,272},{24,280},{32,288},{40,296},{48,304},{56,3... | collective-permute-start | bytes 786440 | tf_op jit(solution)/shard_map/ppermute | solution.py:13
  154.7 15.6 %collective-permute-start.2 = (f32[1,16,32,128]{3,2,1,0:T(8,128)S(1)}, f32[1,16,32,128]{3,2,1,0:T(8,128)S(1)}, u32[]{:S(2)}, u32[]{:S(2)}) collective-permute-start(f32[1,16,32,128]{3,2,1,0:T(8,128)S(1)} %add_multiply_fusion.1), channel_id=1, source_target_pairs={{0,32},{8,40},{16,48},{24,56},{32,0},{40,8},{48,16},{56,24},{64,96... | collective-permute-start | bytes 786440 | tf_op jit(solution)/shard_map/ppermute | solution.py:13
  157.0 58.7 %collective-permute-start.9 = (f32[16,1,128]{2,1,0:T(1,128)S(1)}, f32[16,1,128]{2,1,0:T(1,128)S(1)}, u32[]{:S(2)}, u32[]{:S(2)}) collective-permute-start(f32[16,1,128]{2,1,0:T(1,128)S(1)} %broadcast.113), channel_id=1, source_target_pairs={{32,0},{40,8},{48,16},{56,24},{64,32},{72,40},{80,48},{88,56},{96,... | collective-permute-start | bytes 24584 | tf_op jit(solution)/shard_map/ppermute | solution.py:19
  158.3 57.5 %collective-permute-start.8 = (f32[16,1,128]{2,1,0:T(1,128)S(1)}, f32[16,1,128]{2,1,0:T(1,128)S(1)}, u32[]{:S(2)}, u32[]{:S(2)}) collective-permute-start(f32[16,1,128]{2,1,0:T(1,128)S(1)} %broadcast.113), channel_id=1, source_target_pairs={{0,32},{8,40},{16,48},{24,56},{32,64},{40,72},{48,80},{56,88},{64,... | collective-permute-start | bytes 24584 | tf_op jit(solution)/shard_map/ppermute | solution.py:19
  164.5 45.1 %collective-permute-start.11 = (f32[16,32,1]{2,1,0:T(8,128)}, f32[16,32,1]{2,1,0:T(8,128)}, u32[]{:S(2)}, u32[]{:S(2)}) collective-permute-start(f32[16,32,1]{2,1,0:T(8,128)} %broadcast.114), channel_id=1, source_target_pairs={{8,0},{16,8},{24,16},{32,24},{40,32},{48,40},{56,48},{64,56},{72,6... | collective-permute-start | bytes 6152 | tf_op jit(solution)/shard_map/ppermute | solution.py:19
  165.8 46.7 %collective-permute-start.10 = (f32[16,32,1]{2,1,0:T(8,128)}, f32[16,32,1]{2,1,0:T(8,128)S(1)}, u32[]{:S(2)}, u32[]{:S(2)}) collective-permute-start(f32[16,32,1]{2,1,0:T(8,128)} %broadcast.114), channel_id=1, source_target_pairs={{0,8},{8,16},{16,24},{24,32},{32,40},{40,48},{48,56},{56,64},{64,7... | collective-permute-start | bytes 6152 | tf_op jit(solution)/shard_map/ppermute | solution.py:19
  170.2 33.3 %collective-permute-start.3 = (f32[1,16,32,128]{3,2,1,0:T(8,128)S(1)}, f32[1,16,32,128]{3,2,1,0:T(8,128)S(1)}, u32[]{:S(2)}, u32[]{:S(2)}) collective-permute-start(f32[1,16,32,128]{3,2,1,0:T(8,128)S(1)} %collective-permute-done.2), channel_id=1, source_target_pairs={{0,64},{8,72},{16,80},{24,88},{32,96},{40,104},{48,112},{56,120},{... | collective-permute-start | bytes 786440 | tf_op jit(solution)/shard_map/ppermute | solution.py:13
  203.5 24.7 %collective-permute-start.6 = (f32[1,32,128]{2,1,0:T(8,128)S(1)}, f32[1,32,128]{2,1,0:T(8,128)S(1)}, u32[]{:S(2)}, u32[]{:S(2)}) collective-permute-start(f32[1,32,128]{2,1,0:T(8,128)S(1)} %broadcast.112), channel_id=1, source_target_pairs={{0,128},{8,136},{16,144},{24,152},{32,160},{40,168},{48,176},{56,1... | collective-permute-start | bytes 49160 | tf_op jit(solution)/shard_map/ppermute | solution.py:19
  209.6 4.2 collective-permute-start.4
  212.5 459.1 %collective-permute-start.7 = (f32[1,32,128]{2,1,0:T(8,128)S(1)}, f32[1,32,128]{2,1,0:T(8,128)S(1)}, u32[]{:S(2)}, u32[]{:S(2)}) collective-permute-start(f32[1,32,128]{2,1,0:T(8,128)S(1)} %broadcast.112), channel_id=1, source_target_pairs={{128,0},{136,8},{144,16},{152,24},{160,32},{168,40},{176,48},{184,... | collective-permute-start | bytes 49160 | tf_op jit(solution)/shard_map/ppermute | solution.py:19
  213.8 10.7 %collective-permute-start.5 = (f32[1,16,32,128]{3,2,1,0:T(8,128)S(1)}, f32[1,16,32,128]{3,2,1,0:T(8,128)}, u32[]{:S(2)}, u32[]{:S(2)}) collective-permute-start(f32[1,16,32,128]{3,2,1,0:T(8,128)S(1)} %collective-permute-done.4), channel_id=1, source_target_pairs={{0,16},{8,24},{16,0},{24,8},{32,48},{40,56},{48,32},{56,40},{64,80... | collective-permute-start | bytes 786440 | tf_op jit(solution)/shard_map/ppermute | solution.py:13
  444.4 227.2 %copy-start.3 = (f32[1,16,32,128]{3,2,1,0:T(8,128)}, f32[1,16,32,128]{3,2,1,0:T(8,128)S(1)}, u32[]{:S(2)}) copy-start(f32[1,16,32,128]{3,2,1,0:T(8,128)S(1)} %multiply_subtract_fusion) | copy-start | bytes 786436
  672.5 12.3 %collective-permute-start.16 = (f32[16,32,1]{2,1,0:T(8,128)S(1)}, f32[16,32,1]{2,1,0:T(8,128)S(1)}, u32[]{:S(2)}, u32[]{:S(2)}) collective-permute-start(f32[16,32,1]{2,1,0:T(8,128)S(1)} %get-tuple-element.22), channel_id=1, source_target_pairs={{0,8},{8,16},{16,24},{24,32},{32,40},{40,48},{48,56},{56,64},{64,7... | collective-permute-start | bytes 6152 | tf_op jit(solution)/shard_map/ppermute | solution.py:19
  674.2 12.0 %collective-permute-start.17 = (f32[16,32,1]{2,1,0:T(8,128)S(1)}, f32[16,32,1]{2,1,0:T(8,128)S(1)}, u32[]{:S(2)}, u32[]{:S(2)}) collective-permute-start(f32[16,32,1]{2,1,0:T(8,128)S(1)} %get-tuple-element.23), channel_id=1, source_target_pairs={{8,0},{16,8},{24,16},{32,24},{40,32},{48,40},{56,48},{64,56},{72,6... | collective-permute-start | bytes 6152 | tf_op jit(solution)/shard_map/ppermute | solution.py:19
  675.5 10.7 %collective-permute-start.15 = (f32[16,1,128]{2,1,0:T(1,128)S(1)}, f32[16,1,128]{2,1,0:T(1,128)S(1)}, u32[]{:S(2)}, u32[]{:S(2)}) collective-permute-start(f32[16,1,128]{2,1,0:T(1,128)S(1)} %get-tuple-element.21), channel_id=1, source_target_pairs={{32,0},{40,8},{48,16},{56,24},{64,32},{72,40},{80,48},{88,56},{96,... | collective-permute-start | bytes 24584 | tf_op jit(solution)/shard_map/ppermute | solution.py:19
  676.8 9.4 %collective-permute-start.14 = (f32[16,1,128]{2,1,0:T(1,128)S(1)}, f32[16,1,128]{2,1,0:T(1,128)S(1)}, u32[]{:S(2)}, u32[]{:S(2)}) collective-permute-start(f32[16,1,128]{2,1,0:T(1,128)S(1)} %get-tuple-element.20), channel_id=1, source_target_pairs={{0,32},{8,40},{16,48},{24,56},{32,64},{40,72},{48,80},{56,88},{64,... | collective-permute-start | bytes 24584 | tf_op jit(solution)/shard_map/ppermute | solution.py:19
  682.2 4.0 collective-permute-start.12
  684.8 5.6 collective-permute-start.13
  690.9 21.5 %collective-permute-start.22 = (f32[16,32,1]{2,1,0:T(8,128)S(1)}, f32[16,32,1]{2,1,0:T(8,128)S(1)}, u32[]{:S(2)}, u32[]{:S(2)}) collective-permute-start(f32[16,32,1]{2,1,0:T(8,128)S(1)} %get-tuple-element.16), channel_id=1, source_target_pairs={{0,8},{8,16},{16,24},{24,32},{32,40},{40,48},{48,56},{56,64},{64,7... | collective-permute-start | bytes 6152 | tf_op jit(solution)/shard_map/ppermute | solution.py:19
  692.2 21.5 %collective-permute-start.23 = (f32[16,32,1]{2,1,0:T(8,128)S(1)}, f32[16,32,1]{2,1,0:T(8,128)S(1)}, u32[]{:S(2)}, u32[]{:S(2)}) collective-permute-start(f32[16,32,1]{2,1,0:T(8,128)S(1)} %get-tuple-element.17), channel_id=1, source_target_pairs={{8,0},{16,8},{24,16},{32,24},{40,32},{48,40},{56,48},{64,56},{72,6... | collective-permute-start | bytes 6152 | tf_op jit(solution)/shard_map/ppermute | solution.py:19
  693.5 20.2 %collective-permute-start.21 = (f32[16,1,128]{2,1,0:T(1,128)S(1)}, f32[16,1,128]{2,1,0:T(1,128)S(1)}, u32[]{:S(2)}, u32[]{:S(2)}) collective-permute-start(f32[16,1,128]{2,1,0:T(1,128)S(1)} %get-tuple-element.15), channel_id=1, source_target_pairs={{32,0},{40,8},{48,16},{56,24},{64,32},{72,40},{80,48},{88,56},{96,... | collective-permute-start | bytes 24584 | tf_op jit(solution)/shard_map/ppermute | solution.py:19
  694.8 18.9 %collective-permute-start.20 = (f32[16,1,128]{2,1,0:T(1,128)S(1)}, f32[16,1,128]{2,1,0:T(1,128)S(1)}, u32[]{:S(2)}, u32[]{:S(2)}) collective-permute-start(f32[16,1,128]{2,1,0:T(1,128)S(1)} %get-tuple-element.14), channel_id=1, source_target_pairs={{0,32},{8,40},{16,48},{24,56},{32,64},{40,72},{48,80},{56,88},{64,... | collective-permute-start | bytes 24584 | tf_op jit(solution)/shard_map/ppermute | solution.py:19
  700.4 13.4 %collective-permute-start.18 = (f32[1,32,128]{2,1,0:T(8,128)S(1)}, f32[1,32,128]{2,1,0:T(8,128)S(1)}, u32[]{:S(2)}, u32[]{:S(2)}) collective-permute-start(f32[1,32,128]{2,1,0:T(8,128)S(1)} %get-tuple-element.12), channel_id=1, source_target_pairs={{0,128},{8,136},{16,144},{24,152},{32,160},{40,168},{48,176},{56,1... | collective-permute-start | bytes 49160 | tf_op jit(solution)/shard_map/ppermute | solution.py:19
  712.4 5.6 collective-permute-start.19
  718.5 21.8 %collective-permute-start.28 = (f32[16,32,1]{2,1,0:T(8,128)S(1)}, f32[16,32,1]{2,1,0:T(8,128)S(1)}, u32[]{:S(2)}, u32[]{:S(2)}) collective-permute-start(f32[16,32,1]{2,1,0:T(8,128)S(1)} %get-tuple-element.10), channel_id=1, source_target_pairs={{0,8},{8,16},{16,24},{24,32},{32,40},{40,48},{48,56},{56,64},{64,7... | collective-permute-start | bytes 6152 | tf_op jit(solution)/shard_map/ppermute | solution.py:19
  719.8 21.8 %collective-permute-start.29 = (f32[16,32,1]{2,1,0:T(8,128)S(1)}, f32[16,32,1]{2,1,0:T(8,128)S(1)}, u32[]{:S(2)}, u32[]{:S(2)}) collective-permute-start(f32[16,32,1]{2,1,0:T(8,128)S(1)} %get-tuple-element.11), channel_id=1, source_target_pairs={{8,0},{16,8},{24,16},{32,24},{40,32},{48,40},{56,48},{64,56},{72,6... | collective-permute-start | bytes 6152 | tf_op jit(solution)/shard_map/ppermute | solution.py:19
  721.1 20.5 %collective-permute-start.27 = (f32[16,1,128]{2,1,0:T(1,128)S(1)}, f32[16,1,128]{2,1,0:T(1,128)S(1)}, u32[]{:S(2)}, u32[]{:S(2)}) collective-permute-start(f32[16,1,128]{2,1,0:T(1,128)S(1)} %get-tuple-element.9), channel_id=1, source_target_pairs={{32,0},{40,8},{48,16},{56,24},{64,32},{72,40},{80,48},{88,56},{96,... | collective-permute-start | bytes 24584 | tf_op jit(solution)/shard_map/ppermute | solution.py:19
  722.4 19.3 %collective-permute-start.26 = (f32[16,1,128]{2,1,0:T(1,128)S(1)}, f32[16,1,128]{2,1,0:T(1,128)S(1)}, u32[]{:S(2)}, u32[]{:S(2)}) collective-permute-start(f32[16,1,128]{2,1,0:T(1,128)S(1)} %get-tuple-element.8), channel_id=1, source_target_pairs={{0,32},{8,40},{16,48},{24,56},{32,64},{40,72},{48,80},{56,88},{64,... | collective-permute-start | bytes 24584 | tf_op jit(solution)/shard_map/ppermute | solution.py:19
  727.9 13.8 %collective-permute-start.24 = (f32[1,32,128]{2,1,0:T(8,128)S(1)}, f32[1,32,128]{2,1,0:T(8,128)S(1)}, u32[]{:S(2)}, u32[]{:S(2)}) collective-permute-start(f32[1,32,128]{2,1,0:T(8,128)S(1)} %get-tuple-element.6), channel_id=1, source_target_pairs={{0,128},{8,136},{16,144},{24,152},{32,160},{40,168},{48,176},{56,1... | collective-permute-start | bytes 49160 | tf_op jit(solution)/shard_map/ppermute | solution.py:19
  740.3 5.6 collective-permute-start.25
Sparse Core Ops, SparseCore 0:
  11.8 121.2 all-gather.2
